TPU v7x, 512 devices: a whole 4x4x16 slice. The times are simulated.
512 devices in a mesh: tm: 128 (over x, z, core), head: 4 (over y).
Axes of the slice: x: 4, y: 4, z: 16, core: 2. Of those that a mesh axis runs over, the one named last changes fastest.
Arguments:
- latent: bfloat16 [65536, 1024], P('tm', 'head'), may hold values from -6 to 6
- timestep: int32 [1], replicated, may hold values from 0 to 999
- in_gain: float32 [1024], replicated, may hold values from 0.1 to 1.9
- w_x: bfloat16 [1024, 2048], P(None, 'head'), may hold values from -0.1875 to 0.1875
- w_z: bfloat16 [1024, 2048], P(None, 'head'), may hold values from -0.1875 to 0.1875
- w_bc: bfloat16 [1024, 256], replicated, may hold values from -0.1875 to 0.1875
- w_dt: bfloat16 [1024, 32], P(None, 'head'), may hold values from -0.1875 to 0.1875
- conv_x: float32 [4, 2048], P(None, 'head'), may hold values from -3 to 3
- conv_bc: float32 [4, 256], replicated, may hold values from -3 to 3
- dt_bias: float32 [32], P('head'), may hold values from -1 to 0.5
- a_log: float32 [32], P('head'), may hold values from -13 to -1, as said below
- d_skip: float32 [32], P('head'), may hold values from 4 to 64
- norm_gain: float32 [2048], P('head'), may hold values from 0.1 to 1.9
- w_out: bfloat16 [2048, 1024], P('head'), may hold values from -0.125 to 0.125
- w_mix: bfloat16 [1024, 1024], P(None, 'head'), may hold values from -0.1875 to 0.1875
Outputs:
- denoised: bfloat16 [65536, 1024], P('tm', 'head')
Inputs may be any that keep to these rules, and one draw needn't show every extreme that they name: `a_log`: the logarithm of each head's decay rate.
All inputs are finite; a program needn't handle non-finite values.
Results may differ from a plain program's by a relative error of at most 0.012.
Values may be sent and summed in bfloat16 or wider, within the bound.
A program may use at most 128 MiB of HBM per device.

v0:
```python
import math
import jax
import jax.numpy as jnp
from jax import lax
from jax.sharding import PartitionSpec as P

BLOCK = 256


def from_behind(block, axis, distance):
    devices = range(lax.axis_size(axis))
    route = [(i - distance, i) for i in devices if i - distance in devices]
    return lax.ppermute(block, axis, route)


def prefix(part, axis, combine, identity):
    place = lax.axis_index(axis)
    gathered = jax.tree.map(lambda a: lax.all_gather(a, axis), part)
    state = jax.tree.map(lambda a, e: jnp.zeros_like(a) + jnp.asarray(e, a.dtype), part, identity)

    def one(hop, state):
        return combine(
            state, jax.tree.map(lambda a: lax.dynamic_index_in_dim(a, hop, 0, False), gathered)
        )

    return lax.fori_loop(0, place, one, state)


def sinusoid(timestep, width):
    half = width // 2
    freq = jnp.exp(-math.log(10000.0) * jnp.arange(half, dtype=jnp.float32) / half)
    angle = timestep.astype(jnp.float32)[0] * freq
    return jnp.concatenate([jnp.sin(angle), jnp.cos(angle)])


def causal_conv(rows, rim, kernel):
    padded = jnp.concatenate([rim, rows], axis=0)
    count = rows.shape[0]
    total = jnp.zeros(rows.shape, jnp.float32)
    for k in range(kernel.shape[0]):
        total = total + padded[k : k + count].astype(jnp.float32) * kernel[k]
    return jax.nn.silu(total).astype(jnp.bfloat16)


def block_terms(xa, bmat, cmat, dt, la):
    steps = xa.shape[0]
    cum = jnp.cumsum(la, axis=0)
    scores = jnp.dot(cmat, bmat.T, preferred_element_type=jnp.float32)
    rowid = lax.broadcasted_iota(jnp.int32, (steps, steps), 0)
    colid = lax.broadcasted_iota(jnp.int32, (steps, steps), 1)
    causal = rowid >= colid
    cumt = cum.T
    seg = cumt[:, :, None] - cumt[:, None, :]
    decay = jnp.exp(jnp.where(causal[None], seg, -jnp.inf))
    mixw = (scores[None] * decay * dt.T[:, None, :]).astype(jnp.bfloat16)
    ydiag = jnp.einsum("hij,jhp->ihp", mixw, xa, preferred_element_type=jnp.float32)
    tail = jnp.exp(cum[-1][None, :] - cum) * dt
    weighted = (bmat.astype(jnp.float32)[:, None, :] * tail[:, :, None]).astype(jnp.bfloat16)
    state = jnp.einsum("jhn,jhp->hnp", weighted, xa, preferred_element_type=jnp.float32)
    total = jnp.exp(cum[-1])
    return (ydiag, state, total, cum)


def block_output(ydiag, cum, cmat, hin, xa, d_skip):
    yoff = jnp.einsum(
        "in,hnp->ihp", cmat, hin.astype(jnp.bfloat16), preferred_element_type=jnp.float32
    )
    yoff = yoff * jnp.exp(cum)[:, :, None]
    return ydiag + yoff + d_skip[None, :, None] * xa.astype(jnp.float32)


def combine_states(earlier, later):
    return (earlier[0] * later[0], earlier[1] * later[0][:, None, None] + later[1])


def shards(
    latent,
    timestep,
    in_gain,
    w_x,
    w_z,
    w_bc,
    w_dt,
    conv_x,
    conv_bc,
    dt_bias,
    a_log,
    d_skip,
    norm_gain,
    w_out,
    w_mix,
):
    whole = lax.all_gather(latent, "head", axis=1, tiled=True)
    u = whole.astype(jnp.float32) + sinusoid(timestep, whole.shape[1])[None, :]
    normed = (u * lax.rsqrt(jnp.mean(u * u, axis=1, keepdims=True) + 1e-05) * in_gain).astype(
        jnp.bfloat16
    )
    xs = jnp.dot(normed, w_x, preferred_element_type=jnp.float32).astype(jnp.bfloat16)
    gate = jnp.dot(normed, w_z, preferred_element_type=jnp.float32).astype(jnp.bfloat16)
    bc = jnp.dot(normed, w_bc, preferred_element_type=jnp.float32).astype(jnp.bfloat16)
    dt_raw = jnp.dot(normed, w_dt, preferred_element_type=jnp.float32)
    width = conv_x.shape[0] - 1
    steps_dev = xs.shape[0]
    rim_x, rim_bc = from_behind((xs[steps_dev - width :], bc[steps_dev - width :]), "tm", 1)
    xa = causal_conv(xs, rim_x, conv_x)
    bca = causal_conv(bc, rim_bc, conv_bc)
    state_n = w_bc.shape[1] // 2
    bmat = bca[:, :state_n]
    cmat = bca[:, state_n:]
    dt = jax.nn.softplus(dt_raw + dt_bias)
    la = dt * -jnp.exp(a_log)
    heads = dt.shape[1]
    hdim = xa.shape[1] // heads
    blocks = steps_dev // BLOCK
    xa4 = xa.reshape(blocks, BLOCK, heads, hdim)
    b3 = bmat.reshape(blocks, BLOCK, state_n)
    c3 = cmat.reshape(blocks, BLOCK, state_n)
    dt3 = dt.reshape(blocks, BLOCK, heads)
    la3 = la.reshape(blocks, BLOCK, heads)
    ydiag, states, totals, cums = jax.vmap(block_terms)(xa4, b3, c3, dt3, la3)
    run_decay = jnp.ones((heads,), jnp.float32)
    run_state = jnp.zeros((heads, state_n, hdim), jnp.float32)
    before = []
    for index in range(blocks):
        before.append((run_decay, run_state))
        run_decay, run_state = combine_states(
            (run_decay, run_state), (totals[index], states[index])
        )
    identity = (jnp.ones_like(run_decay), jnp.zeros_like(run_state))
    _, incoming = prefix((run_decay, run_state), "tm", combine_states, identity)
    hins = jnp.stack([incoming * pair[0][:, None, None] + pair[1] for pair in before])
    ys = jax.vmap(block_output, in_axes=(0, 0, 0, 0, 0, None))(ydiag, cums, c3, hins, xa4, d_skip)
    y = ys.reshape(steps_dev, heads * hdim)
    gated = y * jax.nn.silu(gate.astype(jnp.float32))
    square = lax.psum(jnp.sum(gated * gated, axis=1), "head")
    inner = gated.shape[1] * lax.axis_size("head")
    yn = (gated * lax.rsqrt(square[:, None] / inner + 1e-05) * norm_gain).astype(jnp.bfloat16)
    mix_width = w_mix.shape[1]
    col_start = lax.axis_index("head") * mix_width
    share = steps_dev // lax.axis_size("head")
    row_start = lax.axis_index("head") * share
    summed = lax.psum_scatter(
        jnp.dot(yn, w_out, preferred_element_type=jnp.float32),
        "head",
        scatter_dimension=0,
        tiled=True,
    )
    hidden_rows = (lax.dynamic_slice_in_dim(u, row_start, share, 0) + summed).astype(jnp.bfloat16)
    piece = lax.all_gather(hidden_rows, "head", axis=0, tiled=True)
    own = lax.dynamic_slice_in_dim(piece, col_start, mix_width, 1).astype(jnp.float32)
    return (own + jnp.dot(piece, w_mix, preferred_element_type=jnp.float32)).astype(jnp.bfloat16)


def solution(mesh):
    in_specs = (
        P("tm", "head"),
        P(),
        P(),
        P(None, "head"),
        P(None, "head"),
        P(),
        P(None, "head"),
        P(None, "head"),
        P(),
        P("head"),
        P("head"),
        P("head"),
        P("head"),
        P("head", None),
        P(None, "head"),
    )
    out_specs = P("tm", "head")
    return jax.shard_map(shards, mesh=mesh, in_specs=in_specs, out_specs=out_specs, check_vma=False)
```

profile of v0, /device:TPU:2, one launch (start us, length us, event | category | flops | bytes accessed | tf_op | source)
XLA Modules:
  0.0 528.2 jit_solution(13383259743243343161)
XLA Ops:
  10.4 36.6 %all-gather.5.cloned.1.call-done = bf16[512,1024]{1,0:T(8,128)(2,1)} async-done(((bf16[512,256]{1,0:T(8,128)(2,1)}), bf16[512,1024]{1,0:T(8,128)(2,1)}) %all-gather.5.cloned.1.call-update) | async-done | bytes 1048592 | tf_op jit(solution)/shard_map/all_gather | solution.py:93
  47.0 2.9 convert_add_fusion
  50.4 1.2 reduce-window.6
  52.7 1.6 convolution_convert_fusion.2
  54.3 1.9 collective-permute-start.1
  57.0 3.6 collective-permute-start
  63.1 1.0 collective-permute-done
  65.9 1.9 fusion.15
  69.4 76.6 %all-gather = f32[128,1,8]{2,1,0:T(1,128)S(1)} all-gather(f32[1,1,8]{2,1,0:T(1,128)S(1)} %get-tuple-element.98), channel_id=1, replica_groups=mesh['tm'=128,'head'=4] {'tm'}, dimensions={0}, use_global_device_ids=true | all-gather | bytes 4128 | tf_op jit(solution)/shard_map/all_gather | solution.py:18
  146.7 1.1 fusion.35
  147.7 114.8 %all-gather.7.cloned.1.call-done = f32[128,8,128,64]{2,3,1,0:T(8,128)} async-done(((f32[1,8,128,64]{2,3,1,0:T(8,128)}), f32[128,8,128,64]{2,3,1,0:T(8,128)}) %all-gather.7.cloned.1.call-update) | async-done | bytes 33554448 | tf_op jit(solution)/shard_map/all_gather | solution.py:18
  262.6 44.0 %while.12 = (s32[]{:T(128)}, f32[8,128,64]{2,1,0:T(8,128)S(1)}, s32[]{:T(128)}, f32[128,8]{1,0:T(8,128)S(1)}, f32[128,8,128,64]{2,3,1,0:T(8,128)}, /*index=5*/s32[]{:T(128)}, s32[]{:T(128)}, s32[]{:T(128)}) while((s32[]{:T(128)}, f32[8,128,64]{2,1,0:T(8,128)S(1)}, s32[]{:T(128)}, f32[128,8]{1,0:T(8,128)S(1)}, f32[128,8,128,64]{2,3,1,0:T(8,128)}, ...), condition=%wide.region_4.5_spmd, body=%wide.region_3.4_spmd.sunk | while | flops 131077 | bytes 1835231 | solution.py:26
  262.6 1.0 constant_dynamic-slice_fusion.2
  265.4 1.0 constant_dynamic-slice_fusion.2
  307.9 3.0 fusion.9
  310.9 2.0 copy.60
  312.9 1.5 reshape.92
  314.4 2.9 multiply_reduce_fusion.1
  317.2 10.5 %psum.7 = f32[512]{0:T(512)S(1)} all-reduce(f32[512]{0:T(512)S(1)} %get-tuple-element.101), channel_id=1, replica_groups=mesh['tm'=128,'head'=4] {'head'}, use_global_device_ids=true, to_apply=%region_6.7 | all-reduce | flops 512 | bytes 4096 | tf_op jit(solution)/shard_map/psum | solution.py:135
  327.7 2.1 fusion.20
  329.9 155.6 %reduce-scatter.2.cloned.1.call-done = f32[128,1024]{1,0:T(8,128)} async-done(((f32[512,1024]{1,0:T(8,128)}), f32[128,1024]{1,0:T(8,128)}) %reduce-scatter.2.cloned.1.call-update) | async-done | bytes 524304 | tf_op jit(solution)/shard_map/reduce_scatter | solution.py:142
  485.5 2.0 add_convert_fusion
  487.5 31.7 %all-gather.9.cloned.1.call-done = bf16[512,1024]{1,0:T(8,128)(2,1)} async-done(((bf16[128,1024]{1,0:T(8,128)(2,1)}), bf16[512,1024]{1,0:T(8,128)(2,1)}) %all-gather.9.cloned.1.call-update) | async-done | bytes 1048592 | tf_op jit(solution)/shard_map/all_gather | solution.py:149
  519.3 2.4 fusion.10
  (203 shorter events, 53.9 us)
Async XLA Ops:
  6.5 321.2 %copy-start = (bf16[512,1024]{1,0:T(8,128)(2,1)S(1)}, bf16[512,1024]{1,0:T(8,128)(2,1)}, u32[]{:S(2)}) copy-start(bf16[512,1024]{1,0:T(8,128)(2,1)} %param.30) | copy-start | bytes 3145732
  6.5 43.4 %copy-start.14 = (f32[1024]{0:T(1024)S(1)}, f32[1024]{0:T(1024)}, u32[]{:S(2)}) copy-start(f32[1024]{0:T(1024)} %param.19) | copy-start | bytes 12292
  6.5 43.4 %copy-start.13 = (bf16[1024,8]{0,1:T(8,128)(2,1)S(1)}, bf16[1024,8]{0,1:T(8,128)(2,1)}, u32[]{:S(2)}) copy-start(bf16[1024,8]{0,1:T(8,128)(2,1)} %param.23) | copy-start | bytes 49156
  6.5 43.4 %copy-start.16 = (f32[8]{0:T(128)S(1)}, f32[8]{0:T(128)}, u32[]{:S(2)}) copy-start(f32[8]{0:T(128)} %param.26) | copy-start | bytes 100
  6.5 40.5 %all-gather.5.cloned.1.call-start = ((), (), s32[]{:S(2)}) async-start(), calls=%async_computation.1 | async-start | bytes 1310720 | tf_op jit(solution)/shard_map/all_gather | solution.py:93
  7.3 255.3 %all-gather.7.cloned.1.call-start = ((), (), s32[]{:S(2)}) async-start(), calls=%async_computation.2 | async-start | bytes 33816576 | tf_op jit(solution)/shard_map/all_gather | solution.py:18
  47.0 2.9 copy-start.3
  50.4 6.6 %copy-start.6 = (f32[512,8]{0,1:T(8,128)}, f32[512,8]{0,1:T(8,128)S(1)}, u32[]{:S(2)}) copy-start(f32[512,8]{0,1:T(8,128)S(1)} %get-tuple-element.100) | copy-start | bytes 49156
  50.4 5.8 %copy-start.11 = (bf16[1024,512]{1,0:T(8,128)(2,1)S(1)}, bf16[1024,512]{1,0:T(8,128)(2,1)}, u32[]{:S(2)}) copy-start(bf16[1024,512]{1,0:T(8,128)(2,1)} %param.20) | copy-start | bytes 3145732
  54.3 7.0 %collective-permute-start.1 = (bf16[3,256]{1,0:T(4,128)(2,1)S(1)}, bf16[3,256]{1,0:T(4,128)(2,1)S(1)}, u32[]{:S(2)}, u32[]{:S(2)}) collective-permute-start(bf16[3,256]{1,0:T(4,128)(2,1)S(1)} %slice.106), channel_id=1, source_target_pairs={{0,4},{4,8},{8,12},{12,16},{16,20},{20,24},{24,28},{28,32},{32,36}... | collective-permute-start | bytes 4616 | tf_op jit(solution)/shard_map/ppermute | solution.py:13
  57.0 7.0 %collective-permute-start = (bf16[3,512]{1,0:T(4,128)(2,1)S(1)}, bf16[3,512]{1,0:T(4,128)(2,1)S(1)}, u32[]{:S(2)}, u32[]{:S(2)}) collective-permute-start(bf16[3,512]{1,0:T(4,128)(2,1)S(1)} %slice.101), channel_id=1, source_target_pairs={{0,4},{4,8},{8,12},{12,16},{16,20},{20,24},{24,28},{28,32},{32,36}... | collective-permute-start | bytes 9224 | tf_op jit(solution)/shard_map/ppermute | solution.py:13
  65.3 81.4 %copy-start.1 = (bf16[512,128]{1,0:T(8,128)(2,1)S(1)}, bf16[512,128]{1,0:T(8,128)(2,1)}, u32[]{:S(2)}) copy-start(bf16[512,128]{1,0:T(8,128)(2,1)} %get-tuple-element.87) | copy-start | bytes 393220
  68.7 416.9 %reduce-scatter.2.cloned.1.call-start = ((), (), s32[]{:S(2)}) async-start(), calls=%async_computation.3 | async-start | bytes 2621440 | tf_op jit(solution)/shard_map/reduce_scatter | solution.py:142
  306.6 0.9 copy-start.2
  306.6 1.2 copy-start.4
  306.8 1.0 copy-start.5
  306.8 1.0 copy-start.7
  306.8 1.0 copy-start.8
  306.9 1.0 copy-start.9
  312.9 1.5 copy-start.15
  314.4 13.4 %copy-start.10 = (f32[512]{0:T(512)S(1)}, f32[512]{0:T(512)}, u32[]{:S(2)}) copy-start(f32[512]{0:T(512)} %param.29) | copy-start | bytes 6148
  329.9 189.4 %copy-start.12 = (bf16[1024,256]{1,0:T(8,128)(2,1)S(1)}, bf16[1024,256]{1,0:T(8,128)(2,1)}, u32[]{:S(2)}) copy-start(bf16[1024,256]{1,0:T(8,128)(2,1)} %param.31) | copy-start | bytes 1572868
  329.9 189.4 %all-gather.9.cloned.1.call-start = ((), (), s32[]{:S(2)}) async-start(), calls=%async_computation.4 | async-start | bytes 1310720 | tf_op jit(solution)/shard_map/all_gather | solution.py:149
Sparse Core Ops, SparseCore 0:
  9.4 37.5 all-gather.4
  68.8 193.7 all-gather.6
  330.0 155.4 reduce-scatter.1
  487.6 31.5 all-gather.8
where the time goes:
time: 533 us; the launch traced here: 528 us
  waiting for transfers between devices  341 us (64%)
  blocking collectives  87.1 us (16%)
  local copies, waits for them, and re-layouts  46 us (9%)
  matrix products  16.5 us (3%)
  other arithmetic  16.1 us (3%)
  between operations  14.1 us (3%)
  starting transfers between devices  5.65 us (1%)
    reduce_scatter x1, waiting for transfers between devices, shards(): lax.psum_scatter(jnp.dot(yn, w_out, preferred_element_type=jnp.float32),...  156 us
    all_gather x1, waiting for transfers between devices, prefix(): gathered = jax.tree.map(lambda a: lax.all_gather(a, axis), part)  115 us
    all_gather x1, blocking collectives, prefix(): gathered = jax.tree.map(lambda a: lax.all_gather(a, axis), part)  76.6 us
    dynamic_slice x64, local copies, waits for them, and re-layouts, one(): lax.dynamic_index_in_dim(a, hop, 0, False)  37.5 us
    all_gather x1, waiting for transfers between devices, shards(): whole = lax.all_gather(latent, 'head', axis=1, tiled=True)  36.6 us
    all_gather x1, waiting for transfers between devices, shards(): piece = lax.all_gather(hidden_rows, 'head', axis=0, tiled=True)  31.7 us
  transfers between devices with their start and end apart: 6, of which 6 were waited for; matrix products, arithmetic and copies ran while one was open for 1% of the time, Pallas kernels for 0%

commit v1 on v0

--- a/solution.py
+++ b/solution.py
@@ -90,7 +90,24 @@
     w_out,
     w_mix,
 ):
-    whole = lax.all_gather(latent, "head", axis=1, tiled=True)
+    size, index_2, rows_2 = (lax.axis_size("head"), lax.axis_index("head"), latent.shape[1])
+    right = [(i_2, (i_2 + 1) % size) for i_2 in range(size)]
+    left = [(i_2, (i_2 - 1) % size) for i_2 in range(size)]
+    result = jnp.zeros((*latent.shape[:1], size * rows_2, *latent.shape[1 + 1 :]), latent.dtype)
+    result = lax.dynamic_update_slice_in_dim(result, latent, index_2 * rows_2, axis=1)
+    from_left = from_right = latent
+    half_2 = size // 2
+    for turn in range(1, half_2 + 1):
+        from_left = lax.ppermute(from_left, "head", right)
+        result = lax.dynamic_update_slice_in_dim(
+            result, from_left, (index_2 - turn) % size * rows_2, axis=1
+        )
+        if turn < size - half_2:
+            from_right = lax.ppermute(from_right, "head", left)
+            result = lax.dynamic_update_slice_in_dim(
+                result, from_right, (index_2 + turn) % size * rows_2, axis=1
+            )
+    whole = result
     u = whole.astype(jnp.float32) + sinusoid(timestep, whole.shape[1])[None, :]
     normed = (u * lax.rsqrt(jnp.mean(u * u, axis=1, keepdims=True) + 1e-05) * in_gain).astype(
         jnp.bfloat16

time: 533 us -> 514 us (0.964)
  waiting for transfers between devices: 341 us -> 313 us
  starting transfers between devices: 5.65 us -> 15.3 us
    all_gather x1 -> x0, waiting for transfers between devices: 36.6 us -> none  [shards(): whole = lax.all_gather(latent, 'head', axis=1, tiled=True)]
    ppermute x0 -> x3, starting transfers between devices: none -> 9.37 us  [the longest x2 5.8 us: shards(): from_left = lax.ppermute(from_left, 'head', right)]
    ppermute x0 -> x3, waiting for transfers between devices: none -> 8.28 us  [the longest x2 8.28 us: shards(): from_left = lax.ppermute(from_left, 'head', right)]
  transfers between devices with their start and end apart: 6 -> 8, of which waited for: 6 -> 7; matrix products, arithmetic and copies ran while one was open for 1% -> 2% of each run, Pallas kernels for 0% -> 0%
where the time goes in v1:
time: 514 us; the launch traced here: 510 us
  waiting for transfers between devices  313 us (61%)
  blocking collectives  86.4 us (17%)
  local copies, waits for them, and re-layouts  47.2 us (9%)
  matrix products  16.5 us (3%)
  starting transfers between devices  15.3 us (3%)
  other arithmetic  14.9 us (3%)
  between operations  14.3 us (3%)
    reduce_scatter x1, waiting for transfers between devices, shards(): lax.psum_scatter(jnp.dot(yn, w_out, preferred_element_type=jnp.float32),...  156 us
    all_gather x1, waiting for transfers between devices, prefix(): gathered = jax.tree.map(lambda a: lax.all_gather(a, axis), part)  113 us
    all_gather x1, blocking collectives, prefix(): gathered = jax.tree.map(lambda a: lax.all_gather(a, axis), part)  76 us
    dynamic_slice x64, local copies, waits for them, and re-layouts, one(): lax.dynamic_index_in_dim(a, hop, 0, False)  37.5 us
    all_gather x1, waiting for transfers between devices, shards(): piece = lax.all_gather(hidden_rows, 'head', axis=0, tiled=True)  31.8 us
    psum x1, blocking collectives, shards(): square = lax.psum(jnp.sum(gated * gated, axis=1), 'head')  10.5 us
  transfers between devices with their start and end apart: 8, of which 7 were waited for; matrix products, arithmetic and copies ran while one was open for 2% of the time, Pallas kernels for 0%

profile of v1, /device:TPU:2, one launch (start us, length us, event | category | flops | bytes accessed | tf_op | source)
XLA Modules:
  0.0 509.5 jit_solution(8961709530280016243)
XLA Ops:
  6.5 3.6 collective-permute-start
  10.2 3.6 collective-permute-start.1
  18.1 2.2 collective-permute-start.2
  20.5 8.1 %collective-permute-done.2 = bf16[512,256]{1,0:T(8,128)(2,1)S(1)} collective-permute-done((bf16[512,256]{1,0:T(8,128)(2,1)S(1)}, bf16[512,256]{1,0:T(8,128)(2,1)S(1)}, u32[]{:S(2)}, u32[]{:S(2)}) %collective-permute-start.2) | collective-permute-done | bytes 262176 | tf_op jit(solution)/shard_map/ppermute | solution.py:101
  28.6 1.6 convert_add_fusion
  30.8 1.2 reduce-window.6
  33.1 1.5 convolution_convert_fusion.2
  34.6 1.9 collective-permute-start.4
  37.4 3.9 collective-permute-start.3
  41.4 3.9 collective-permute-done.4
  49.8 1.9 fusion.15
  53.3 76.0 %all-gather = f32[128,1,8]{2,1,0:T(1,128)S(1)} all-gather(f32[1,1,8]{2,1,0:T(1,128)S(1)} %get-tuple-element.98), channel_id=1, replica_groups=mesh['tm'=128,'head'=4] {'tm'}, dimensions={0}, use_global_device_ids=true | all-gather | bytes 4128 | tf_op jit(solution)/shard_map/all_gather | solution.py:18
  131.0 112.8 %all-gather.4.cloned.1.call-done = f32[128,8,128,64]{2,3,1,0:T(8,128)} async-done(((f32[1,8,128,64]{2,3,1,0:T(8,128)}), f32[128,8,128,64]{2,3,1,0:T(8,128)}) %all-gather.4.cloned.1.call-update) | async-done | bytes 33554448 | tf_op jit(solution)/shard_map/all_gather | solution.py:18
  243.9 44.0 %while.12 = (s32[]{:T(128)}, f32[8,128,64]{2,1,0:T(8,128)S(1)}, s32[]{:T(128)}, f32[128,8]{1,0:T(8,128)S(1)}, f32[128,8,128,64]{2,3,1,0:T(8,128)}, /*index=5*/s32[]{:T(128)}, s32[]{:T(128)}, s32[]{:T(128)}) while((s32[]{:T(128)}, f32[8,128,64]{2,1,0:T(8,128)S(1)}, s32[]{:T(128)}, f32[128,8]{1,0:T(8,128)S(1)}, f32[128,8,128,64]{2,3,1,0:T(8,128)}, ...), condition=%wide.region_4.5_spmd, body=%wide.region_3.4_spmd.sunk | while | flops 131077 | bytes 1835231 | solution.py:26
  289.2 3.0 fusion.9
  292.2 2.0 copy.60
  294.2 1.5 reshape.92
  295.7 2.9 multiply_reduce_fusion.1
  298.6 10.5 %psum.7 = f32[512]{0:T(512)S(1)} all-reduce(f32[512]{0:T(512)S(1)} %get-tuple-element.101), channel_id=1, replica_groups=mesh['tm'=128,'head'=4] {'head'}, use_global_device_ids=true, to_apply=%region_6.7 | all-reduce | flops 512 | bytes 4096 | tf_op jit(solution)/shard_map/psum | solution.py:152
  309.1 2.1 fusion.20
  311.2 155.6 %reduce-scatter.2.cloned.1.call-done = f32[128,1024]{1,0:T(8,128)} async-done(((f32[512,1024]{1,0:T(8,128)}), f32[128,1024]{1,0:T(8,128)}) %reduce-scatter.2.cloned.1.call-update) | async-done | bytes 524304 | tf_op jit(solution)/shard_map/reduce_scatter | solution.py:159
  466.8 2.0 add_convert_fusion
  468.8 31.8 %all-gather.6.cloned.1.call-done = bf16[512,1024]{1,0:T(8,128)(2,1)} async-done(((bf16[128,1024]{1,0:T(8,128)(2,1)}), bf16[512,1024]{1,0:T(8,128)(2,1)}) %all-gather.6.cloned.1.call-update) | async-done | bytes 1048592 | tf_op jit(solution)/shard_map/all_gather | solution.py:166
  500.6 2.4 fusion.10
  (211 shorter events, 57.8 us)
Async XLA Ops:
  6.5 302.5 %copy-start = (bf16[512,1024]{1,0:T(8,128)(2,1)S(1)}, bf16[512,1024]{1,0:T(8,128)(2,1)}, u32[]{:S(2)}) copy-start(bf16[512,1024]{1,0:T(8,128)(2,1)} %param.30) | copy-start | bytes 3145732
  6.5 237.3 %all-gather.4.cloned.1.call-start = ((), (), s32[]{:S(2)}) async-start(), calls=%async_computation.1 | async-start | bytes 33816576 | tf_op jit(solution)/shard_map/all_gather | solution.py:18
  6.5 11.6 %collective-permute-start = (bf16[512,256]{1,0:T(8,128)(2,1)}, bf16[512,256]{1,0:T(8,128)(2,1)S(1)}, u32[]{:S(2)}, u32[]{:S(2)}) collective-permute-start(bf16[512,256]{1,0:T(8,128)(2,1)} %param.17), channel_id=1, source_target_pairs={{0,1},{1,2},{2,3},{3,0},{4,5},{5,6},{6,7},{7,4},{8,9},{9,10},{10,1... | collective-permute-start | bytes 786440 | tf_op jit(solution)/shard_map/ppermute | solution.py:101
  10.2 10.3 %collective-permute-start.1 = (bf16[512,256]{1,0:T(8,128)(2,1)}, bf16[512,256]{1,0:T(8,128)(2,1)S(1)}, u32[]{:S(2)}, u32[]{:S(2)}) collective-permute-start(bf16[512,256]{1,0:T(8,128)(2,1)} %param.17), channel_id=1, source_target_pairs={{0,3},{1,0},{2,1},{3,2},{4,7},{5,4},{6,5},{7,6},{8,11},{9,8},{10,9... | collective-permute-start | bytes 786440 | tf_op jit(solution)/shard_map/ppermute | solution.py:106
  18.1 10.5 %collective-permute-start.2 = (bf16[512,256]{1,0:T(8,128)(2,1)S(1)}, bf16[512,256]{1,0:T(8,128)(2,1)S(1)}, u32[]{:S(2)}, u32[]{:S(2)}) collective-permute-start(bf16[512,256]{1,0:T(8,128)(2,1)S(1)} %collective-permute-done), channel_id=1, source_target_pairs={{0,1},{1,2},{2,3},{3,0},{4,5},{5,6},{6,7},{7,4},{8,9},{9,10},{10,1... | collective-permute-start | bytes 786440 | tf_op jit(solution)/shard_map/ppermute | solution.py:101
  20.4 9.9 %copy-start.13 = (bf16[1024,8]{0,1:T(8,128)(2,1)S(1)}, bf16[1024,8]{0,1:T(8,128)(2,1)}, u32[]{:S(2)}) copy-start(bf16[1024,8]{0,1:T(8,128)(2,1)} %param.23) | copy-start | bytes 49156
  20.4 9.9 %copy-start.14 = (f32[1024]{0:T(1024)S(1)}, f32[1024]{0:T(1024)}, u32[]{:S(2)}) copy-start(f32[1024]{0:T(1024)} %param.19) | copy-start | bytes 12292
  20.4 9.9 %copy-start.16 = (f32[8]{0:T(128)S(1)}, f32[8]{0:T(128)}, u32[]{:S(2)}) copy-start(f32[8]{0:T(128)} %param.26) | copy-start | bytes 100
  28.6 8.0 %copy-start.1 = (bf16[512,1024]{1,0:T(8,128)(2,1)}, bf16[512,1024]{1,0:T(8,128)(2,1)S(1)}, u32[]{:S(2)}) copy-start(bf16[512,1024]{1,0:T(8,128)(2,1)S(1)} %constant_dynamic-update-slice_fusion) | copy-start | bytes 3145732
  30.8 6.6 %copy-start.6 = (f32[512,8]{0,1:T(8,128)}, f32[512,8]{0,1:T(8,128)S(1)}, u32[]{:S(2)}) copy-start(f32[512,8]{0,1:T(8,128)S(1)} %get-tuple-element.100) | copy-start | bytes 49156
  30.8 5.8 %copy-start.11 = (bf16[1024,512]{1,0:T(8,128)(2,1)S(1)}, bf16[1024,512]{1,0:T(8,128)(2,1)}, u32[]{:S(2)}) copy-start(bf16[1024,512]{1,0:T(8,128)(2,1)} %param.20) | copy-start | bytes 3145732
  34.6 10.6 %collective-permute-start.4 = (bf16[3,256]{1,0:T(4,128)(2,1)S(1)}, bf16[3,256]{1,0:T(4,128)(2,1)S(1)}, u32[]{:S(2)}, u32[]{:S(2)}) collective-permute-start(bf16[3,256]{1,0:T(4,128)(2,1)S(1)} %slice.106), channel_id=1, source_target_pairs={{0,4},{4,8},{8,12},{12,16},{16,20},{20,24},{24,28},{28,32},{32,36}... | collective-permute-start | bytes 4616 | tf_op jit(solution)/shard_map/ppermute | solution.py:13
  37.4 10.6 %collective-permute-start.3 = (bf16[3,512]{1,0:T(4,128)(2,1)S(1)}, bf16[3,512]{1,0:T(4,128)(2,1)S(1)}, u32[]{:S(2)}, u32[]{:S(2)}) collective-permute-start(bf16[3,512]{1,0:T(4,128)(2,1)S(1)} %slice.101), channel_id=1, source_target_pairs={{0,4},{4,8},{8,12},{12,16},{16,20},{20,24},{24,28},{28,32},{32,36}... | collective-permute-start | bytes 9224 | tf_op jit(solution)/shard_map/ppermute | solution.py:13
  49.2 80.7 %copy-start.2 = (bf16[512,128]{1,0:T(8,128)(2,1)S(1)}, bf16[512,128]{1,0:T(8,128)(2,1)}, u32[]{:S(2)}) copy-start(bf16[512,128]{1,0:T(8,128)(2,1)} %get-tuple-element.87) | copy-start | bytes 393220
  52.6 414.2 %reduce-scatter.2.cloned.1.call-start = ((), (), s32[]{:S(2)}) async-start(), calls=%async_computation.2 | async-start | bytes 2621440 | tf_op jit(solution)/shard_map/reduce_scatter | solution.py:159
  287.9 1.2 copy-start.4
  288.1 1.0 copy-start.5
  288.1 1.0 copy-start.7
  288.2 1.0 copy-start.8
  288.2 1.0 copy-start.9
  294.2 1.5 copy-start.15
  295.7 13.4 %copy-start.10 = (f32[512]{0:T(512)S(1)}, f32[512]{0:T(512)}, u32[]{:S(2)}) copy-start(f32[512]{0:T(512)} %param.29) | copy-start | bytes 6148
  311.2 189.4 %copy-start.12 = (bf16[1024,256]{1,0:T(8,128)(2,1)S(1)}, bf16[1024,256]{1,0:T(8,128)(2,1)}, u32[]{:S(2)}) copy-start(bf16[1024,256]{1,0:T(8,128)(2,1)} %param.31) | copy-start | bytes 1572868
  311.2 189.4 %all-gather.6.cloned.1.call-start = ((), (), s32[]{:S(2)}) async-start(), calls=%async_computation.3 | async-start | bytes 1310720 | tf_op jit(solution)/shard_map/all_gather | solution.py:166
  (1 other events, 0.9 us)
Sparse Core Ops, SparseCore 0:
  52.7 191.0 all-gather.3
  311.3 155.4 reduce-scatter.1
  468.9 31.5 all-gather.5
